TPU v7x, 32 devices: a whole 2x2x4 slice. The times are simulated.
32 devices in a mesh: dp: 8 (over z, x), tensor: 4 (over y, core).
Axes of the slice: x: 2, y: 2, z: 4, core: 2. Of those that a mesh axis runs over, the one named last changes fastest.
Arguments:
- tokens: bfloat16 [3072, 2048], P('dp', 'tensor'), may hold values from -6 to 6
- partner_bits: int32 [4, 2], replicated, may hold values from 0 to 1, as said below
- w_up: bfloat16 [4, 3, 512, 1024], P('tensor', None, 'dp'), may hold values from -0.15625 to 0.15625
- w_down: bfloat16 [4, 3, 1024, 512], P('tensor', None, 'dp'), may hold values from -0.109375 to 0.109375
Outputs:
- mixed: bfloat16 [3072, 2048], P('dp', 'tensor')
Inputs may be any that keep to these rules, and one draw needn't show every extreme that they name: Each row of partner_bits lists each of 0 to 1 exactly once.
All inputs are finite; a program needn't handle non-finite values.
Results may differ from a plain program's by a relative error of at most 0.0057.
Values may be sent and summed in bfloat16 or wider, within the bound.
A program may use at most 64 MiB of HBM per device.

v0:
```python
import jax
import jax.numpy as jnp
from jax import lax
from jax.sharding import PartitionSpec as P


def swapped(block, axis, bit):
    count = lax.axis_size(axis)
    route = []
    for low in range(count):
        high = low | 1 << bit
        if high != low and high < count:
            route += [(low, high), (high, low)]
    return lax.ppermute(block, axis, route)


def on_device(tokens, partner_bits, w_up, w_down):
    me_index = lax.axis_index("tensor")
    nbits = lax.axis_size("tensor").bit_length() - 1
    select = (jnp.arange(partner_bits.shape[0], dtype=jnp.int32) == me_index).astype(jnp.int32)
    my_bits = jnp.sum(partner_bits * select[:, None], axis=0)
    onehot = (my_bits[:, None] == jnp.arange(nbits, dtype=jnp.int32)[None, :]).astype(jnp.bfloat16)
    bit_list = list(range(nbits))
    received = [None] * nbits
    for bit in bit_list:
        received[bit] = swapped(tokens, "tensor", bit)
    by_bit = jnp.stack(received, axis=0)
    by_slot = jnp.einsum("sk,ktd->std", onehot, by_bit, preferred_element_type=jnp.float32).astype(
        jnp.bfloat16
    )
    inputs = jnp.concatenate([tokens[None], by_slot], axis=0)
    columns = inputs
    pre = jnp.einsum(
        "std,sdf->tf",
        columns,
        lax.all_gather(w_up, "dp", axis=2, tiled=True)[0],
        preferred_element_type=jnp.float32,
    )
    hidden = jax.nn.gelu(pre, approximate=True).astype(jnp.bfloat16)
    columns = hidden
    terms = jnp.einsum(
        "tf,sfd->std",
        columns,
        lax.all_gather(w_down, "dp", axis=2, tiled=True)[0],
        preferred_element_type=jnp.float32,
    )
    terms = terms.astype(jnp.bfloat16)
    owed = jnp.einsum("sk,std->ktd", onehot, terms[1:], preferred_element_type=jnp.float32).astype(
        jnp.bfloat16
    )
    total = terms[0].astype(jnp.float32)
    for bit in bit_list:
        total = total + swapped(owed[bit], "tensor", bit).astype(jnp.float32)
    return total.astype(jnp.bfloat16)


def solution(mesh):
    in_specs = (
        P("dp", "tensor"),
        P(),
        P("tensor", None, "dp", None),
        P("tensor", None, "dp", None),
    )
    out_specs = P("dp", "tensor")
    return jax.shard_map(
        on_device, mesh=mesh, in_specs=in_specs, out_specs=out_specs, check_vma=False
    )
```

profile of v0, /device:TPU:0, one launch (start us, length us, event | category | flops | bytes accessed | tf_op | source)
XLA Modules:
  0.0 159.3 jit_solution(11374024917748464835)
XLA Ops:
  6.5 0.0 all-gather.3.cloned.1.call-start
  6.5 0.7 all-gather.3.cloned.1.call-update
  7.3 0.0 all-gather.5.cloned.1.call-start
  7.3 0.7 all-gather.5.cloned.1.call-update
  8.0 3.1 %collective-permute-start.1 = (bf16[384,512]{1,0:T(8,128)(2,1)}, bf16[384,512]{1,0:T(8,128)(2,1)S(1)}, u32[]{:S(2)}, u32[]{:S(2)}) collective-permute-start(bf16[384,512]{1,0:T(8,128)(2,1)} %param.4), channel_id=1, source_target_pairs={{0,2},{2,0},{1,3},{3,1},{4,6},{6,4},{5,7},{7,5},{8,10},{10,8},{9,1... | collective-permute-start | bytes 1179656 | tf_op jit(solution)/shard_map/ppermute | solution.py:14
  11.1 0.0 collective-permute-start
  11.1 0.8 multiply_reduce_fusion
  11.9 8.5 %collective-permute-done.1 = bf16[384,512]{1,0:T(8,128)(2,1)S(1)} collective-permute-done((bf16[384,512]{1,0:T(8,128)(2,1)}, bf16[384,512]{1,0:T(8,128)(2,1)S(1)}, u32[]{:S(2)}, u32[]{:S(2)}) %collective-permute-start.1) | collective-permute-done | bytes 393248 | tf_op jit(solution)/shard_map/ppermute | solution.py:14
  20.4 0.0 collective-permute-done
  20.4 0.1 pad_maximum_fusion
  20.5 1.4 fusion.36
  21.9 0.0 copy-start
  21.9 0.1 copy.15
  22.0 50.3 %all-gather.3.cloned.1.call-done = bf16[1,3,512,1024]{3,2,1,0:T(8,128)(2,1)} async-done(((bf16[1,3,64,1024]{3,2,1,0:T(8,128)(2,1)}), bf16[1,3,512,1024]{3,2,1,0:T(8,128)(2,1)}) %all-gather.3.cloned.1.call-update) | async-done | bytes 3145744 | tf_op jit(solution)/shard_map/all_gather | solution.py:36
  72.3 60.9 %all-gather.5.cloned.1.call-done = bf16[1,3,1024,512]{3,2,1,0:T(8,128)(2,1)} async-done(((bf16[1,3,128,512]{3,2,1,0:T(8,128)(2,1)}), bf16[1,3,1024,512]{3,2,1,0:T(8,128)(2,1)}) %all-gather.5.cloned.1.call-update) | async-done | bytes 3145744 | tf_op jit(solution)/shard_map/all_gather | solution.py:44
  133.2 0.0 copy-done
  133.2 5.6 %fusion.17 = bf16[3,384,512]{2,1,0:T(8,128)(2,1)S(1)} fusion(bf16[1,3,1024,512]{3,2,1,0:T(8,128)(2,1)} %all-gather.5.cloned.1.call-done, bf16[1,3,512,1024]{3,2,1,0:T(8,128)(2,1)} %all-gather.3.cloned.1.call-done, bf16[2,384,512]{2,1,0:T(8,128)(2,1)S(1)} %copy.15, bf16[1,384,512]{2,1,0:T(8,128)(2,1)S(1)} %bitcast.46), kind=kOutput, calls=%fused_computation.16 | convolution fusion | flops 2420637696 | bytes 8650752 | tf_op jit(solution)/shard_map/tf,sfd->std/dot_general | solution.py:41
  138.8 0.1 slice.17
  138.8 1.0 fusion.38
  139.8 0.1 copy.16
  139.9 0.1 slice_bitcast_fusion.1
  140.0 0.1 collective-permute-start.2
  140.0 1.5 collective-permute-start.3
  141.6 0.2 collective-permute-done.2
  141.8 9.8 %collective-permute-done.3 = bf16[384,512]{1,0:T(8,128)(2,1)S(1)} collective-permute-done((bf16[384,512]{1,0:T(8,128)(2,1)S(1)}, bf16[384,512]{1,0:T(8,128)(2,1)S(1)}, u32[]{:S(2)}, u32[]{:S(2)}) %collective-permute-start.3) | collective-permute-done | bytes 393248 | tf_op jit(solution)/shard_map/ppermute | solution.py:14
  151.6 0.9 fusion.31
  (1 shorter events, 0.0 us)
Async XLA Ops:
  6.5 65.8 %all-gather.3.cloned.1.call-start = ((), (), s32[]{:S(2)}) async-start(), calls=%async_computation | async-start | bytes 3538944 | tf_op jit(solution)/shard_map/all_gather | solution.py:36
  7.3 125.9 %all-gather.5.cloned.1.call-start = ((), (), s32[]{:S(2)}) async-start(), calls=%async_computation.1 | async-start | bytes 3538944 | tf_op jit(solution)/shard_map/all_gather | solution.py:44
  8.0 12.4 %collective-permute-start.1 = (bf16[384,512]{1,0:T(8,128)(2,1)}, bf16[384,512]{1,0:T(8,128)(2,1)S(1)}, u32[]{:S(2)}, u32[]{:S(2)}) collective-permute-start(bf16[384,512]{1,0:T(8,128)(2,1)} %param.4), channel_id=1, source_target_pairs={{0,2},{2,0},{1,3},{3,1},{4,6},{6,4},{5,7},{7,5},{8,10},{10,8},{9,1... | collective-permute-start | bytes 1179656 | tf_op jit(solution)/shard_map/ppermute | solution.py:14
  11.1 9.3 %collective-permute-start = (bf16[384,512]{1,0:T(8,128)(2,1)}, bf16[384,512]{1,0:T(8,128)(2,1)S(1)}, u32[]{:S(2)}, u32[]{:S(2)}) collective-permute-start(bf16[384,512]{1,0:T(8,128)(2,1)} %param.4), channel_id=1, source_target_pairs={{0,1},{1,0},{2,3},{3,2},{4,5},{5,4},{6,7},{7,6},{8,9},{9,8},{10,11... | collective-permute-start | bytes 1179656 | tf_op jit(solution)/shard_map/ppermute | solution.py:14
  21.9 111.3 %copy-start = (bf16[384,512]{1,0:T(8,128)(2,1)S(1)}, bf16[384,512]{1,0:T(8,128)(2,1)}, u32[]{:S(2)}) copy-start(bf16[384,512]{1,0:T(8,128)(2,1)} %param.4) | copy-start | bytes 1179652
  140.0 1.8 %collective-permute-start.2 = (bf16[384,512]{1,0:T(8,128)(2,1)S(1)}, bf16[384,512]{1,0:T(8,128)(2,1)S(1)}, u32[]{:S(2)}, u32[]{:S(2)}) collective-permute-start(bf16[384,512]{1,0:T(8,128)(2,1)S(1)} %get-tuple-element.5), channel_id=1, source_target_pairs={{0,1},{1,0},{2,3},{3,2},{4,5},{5,4},{6,7},{7,6},{8,9},{9,8},{10,11... | collective-permute-start | bytes 1179656 | tf_op jit(solution)/shard_map/ppermute | solution.py:14
  140.0 11.5 %collective-permute-start.3 = (bf16[384,512]{1,0:T(8,128)(2,1)S(1)}, bf16[384,512]{1,0:T(8,128)(2,1)S(1)}, u32[]{:S(2)}, u32[]{:S(2)}) collective-permute-start(bf16[384,512]{1,0:T(8,128)(2,1)S(1)} %get-tuple-element.6), channel_id=1, source_target_pairs={{0,2},{2,0},{1,3},{3,1},{4,6},{6,4},{5,7},{7,5},{8,10},{10,8},{9,1... | collective-permute-start | bytes 1179656 | tf_op jit(solution)/shard_map/ppermute | solution.py:14
Sparse Core Ops, SparseCore 0:
  9.5 62.7 all-gather.2
  74.5 58.6 all-gather.4
where the time goes:
time: 159 us
  waiting for transfers between devices  131 us (82%)
  between operations  13.5 us (8%)
  matrix products  7.96 us (5%)
  starting transfers between devices  4.71 us (3%)
  other arithmetic  1.77 us (1%)
    all_gather x1, waiting for transfers between devices, on_device(): lax.all_gather(w_down, 'dp', axis=2, tiled=True)[0]  60.9 us
    all_gather x1, waiting for transfers between devices, on_device(): lax.all_gather(w_up, 'dp', axis=2, tiled=True)[0]  50.3 us
    ppermute x4, waiting for transfers between devices, swapped(): return lax.ppermute(block, axis, route)  18.5 us
    dot_general x1, matrix products, on_device(): jnp.einsum('tf,sfd->std', columns, lax.all_gather(w_down, 'dp', axis=2, t...  5.59 us
    ppermute x4, starting transfers between devices, swapped(): return lax.ppermute(block, axis, route)  4.67 us
  transfers between devices with their start and end apart: 6, of which 5 were waited for; matrix products, arithmetic and copies ran while one was open for 1% of the time, Pallas kernels for 0%

commit v1 on v0

v1 whole, which is shorter than its diff:
```python
import functools

import jax
import jax.numpy as jnp
from jax import lax
from jax.experimental import pallas as pl
from jax.experimental.pallas import tpu as pltpu
from jax.sharding import PartitionSpec as P

MESH = pl.DeviceIdType.MESH
OWN_CHUNKS = 2


def item_list(slots, width):
    items = [("up", 0, 0, 0), ("up", 1, 0, 0)]
    for slot in range(slots - 1, 0, -1):
        items.append(("down", slot, 0, width))
    part = width // OWN_CHUNKS
    for chunk in range(OWN_CHUNKS):
        items.append(("down", 0, chunk * part, part))
    return items


def kernel(
    nz, items, tok_ref, up_ref, down_ref, out_ref,
    tok, up, down, hid, stage, landed, own,
    line_send, line_recv, local_sem, side_send, side_recv,
    tok_send, tok_recv, term_send, term_recv,
):
    slots = tok.shape[0]
    rows_up, rows_down = up_ref.shape[2], down_ref.shape[1]
    me, rank = lax.axis_index("dp"), lax.axis_index("tensor")
    z, x = me // 2, me % 2
    other = z * 2 + (1 - x)
    partner = [rank]
    for bit in range(slots - 1):
        partner.append(rank + (1 - 2 * ((rank // (1 << bit)) % 2)) * (1 << bit))

    barrier = pltpu.get_barrier_semaphore()
    greeted = [((((z + 1) % nz) * 2 + x), rank), (((z + nz - 1) % nz) * 2 + x, rank), (other, rank)]
    for slot in range(1, slots):
        greeted += [(me, partner[slot]), (other, partner[slot])]
    for device in greeted:
        pl.semaphore_signal(barrier, inc=1, device_id=device, device_id_type=MESH)
    pl.semaphore_wait(barrier, len(greeted))

    def up_rows(at_z, at_x):
        return up.at[:, pl.ds(pl.multiple_of((at_z * 2 + at_x) * rows_up, rows_up), rows_up), :]

    def place(item, at_z):
        kind, which, first, width = item
        if kind == "up":
            return up_rows(at_z, x if which == 0 else 1 - x)
        row = pl.multiple_of(at_z * rows_down, rows_down)
        return down.at[which, pl.ds(row, rows_down), pl.ds(first, width)]

    def source(item, hop, at_z):
        kind, which, first, width = item
        if hop > 1 or (kind == "up" and which == 1):
            return place(item, at_z)
        if kind == "up":
            return up_ref.at[x]
        return down_ref.at[which, :, pl.ds(first, width)]

    def line(i, hop, way):
        sign = 1 - 2 * way
        origin = z - sign * (hop - 1)
        return pltpu.make_async_remote_copy(
            src_ref=source(items[i], hop, origin),
            dst_ref=place(items[i], origin),
            send_sem=line_send.at[i, way, hop - 1],
            recv_sem=line_recv.at[i, way, hop - 1],
            device_id=((z + sign) * 2 + x, rank),
            device_id_type=MESH,
        )

    def sends(hop, way):
        if way == 0:
            return jnp.logical_and(z - (hop - 1) >= 0, z < nz - 1)
        return jnp.logical_and(z + (hop - 1) < nz, z > 0)

    def receives(hop, way):
        return z - hop >= 0 if way == 0 else z + hop < nz

    def send(i, hop):
        for way in (0, 1):
            @pl.when(sends(hop, way))
            def _():
                line(i, hop, way).start()

    def sent(i, hop):
        for way in (0, 1):
            @pl.when(sends(hop, way))
            def _():
                line(i, hop, way).wait_send()

    def arrive(i, hop):
        for way in (0, 1):
            @pl.when(receives(hop, way))
            def _():
                origin = z - (1 - 2 * way) * hop
                pltpu.make_async_remote_copy(
                    src_ref=place(items[i], origin),
                    dst_ref=place(items[i], origin),
                    send_sem=line_send.at[i, way, hop - 1],
                    recv_sem=line_recv.at[i, way, hop - 1],
                    device_id=(me, rank),
                    device_id_type=MESH,
                ).wait_recv()

    def side(dst_x):
        return pltpu.make_async_remote_copy(
            src_ref=up_ref.at[1 - x], dst_ref=up_rows(z, dst_x),
            send_sem=side_send, recv_sem=side_recv,
            device_id=(other, rank), device_id_type=MESH,
        )

    def token_copy(slot, half):
        at = x if half == 0 else 1 - x
        src = tok_ref if half == 0 else tok.at[0, at]
        return pltpu.make_async_remote_copy(
            src_ref=src, dst_ref=tok.at[slot, at],
            send_sem=tok_send.at[slot, half], recv_sem=tok_recv.at[slot, half],
            device_id=(me, partner[slot]), device_id_type=MESH,
        )

    def token_side():
        return pltpu.make_async_remote_copy(
            src_ref=tok_ref, dst_ref=tok.at[0, x],
            send_sem=tok_send.at[0, 0], recv_sem=tok_recv.at[0, 0],
            device_id=(other, rank), device_id_type=MESH,
        )

    def term_copy(i, far):
        unused, slot, first, width = items[i]
        columns = pl.ds(first, width)
        return pltpu.make_async_remote_copy(
            src_ref=stage.at[slot, 1 - x if far else x, :, columns],
            dst_ref=landed.at[slot, x, :, columns],
            send_sem=term_send.at[i, far], recv_sem=term_recv.at[i, far],
            device_id=(other if far else me, partner[slot]), device_id_type=MESH,
        )

    last = nz - 1
    send(0, 1)
    side(x).start()
    token_side().start()
    for slot in range(slots - 1, 0, -1):
        token_copy(slot, 0).start()
    mine = [
        pltpu.make_async_copy(tok_ref, tok.at[0, x], local_sem.at[0]),
        pltpu.make_async_copy(up_ref.at[x], up_rows(z, x), local_sem.at[1]),
        pltpu.make_async_copy(
            down_ref, down.at[:, pl.ds(pl.multiple_of(z * rows_down, rows_down), rows_down), :], local_sem.at[2]
        ),
    ]
    for copy in mine:
        copy.start()

    def make_hidden():
        for copy in mine:
            copy.wait()
        for slot in range(1, slots):
            for half in (0, 1):
                token_copy(slot, half).wait_recv()

        def one(half, carry):
            pre = jnp.dot(tok[0, half], up[0], preferred_element_type=jnp.float32)
            for slot in range(1, slots):
                pre += jnp.dot(tok[slot, half], up[slot], preferred_element_type=jnp.float32)
            hid[half] = jax.nn.gelu(pre, approximate=True).astype(hid.dtype)
            return carry

        lax.fori_loop(0, 2, one, 0)

    def make_terms(i):
        unused, slot, first, width = items[i]
        columns = slice(first, first + width)

        def term(half):
            return jnp.dot(hid[half], down[slot, :, columns], preferred_element_type=jnp.float32)

        stage[slot, 1 - x, :, columns] = term(1 - x).astype(stage.dtype)
        term_copy(i, 1).start()
        if slot == 0:
            own[:, columns] = term(x)
        else:
            stage[slot, x, :, columns] = term(x).astype(stage.dtype)
            term_copy(i, 0).start()

    count = len(items)
    for step in range(count + last):
        for hop in range(1, nz + 1):
            i = step - (hop - 1)
            if not 0 <= i < count:
                continue
            if hop > 1:
                arrive(i, hop - 1)
            elif i == 1:
                side(1 - x).wait_recv()
            if hop < nz:
                if (i, hop) != (0, 1):
                    send(i, hop)
        if step == 1:
            token_side().wait_recv()
            for slot in range(slots - 1, 0, -1):
                token_copy(slot, 1).start()
        i = step - last
        if i == 1:
            make_hidden()
        if i > 1:
            make_terms(i)

    for i in range(2, count):
        unused, slot, first, width = items[i]
        term_copy(i, 1).wait_recv()
        if slot:
            term_copy(i, 0).wait_recv()
            continue
        columns = slice(first, first + width)
        total = own[:, columns] + landed[0, 1 - x, :, columns].astype(jnp.float32)
        for slot in range(1, slots):
            for half in (0, 1):
                total += landed[slot, half, :, columns].astype(jnp.float32)
        out_ref[:, columns] = total.astype(out_ref.dtype)

    side(x).wait_send()
    token_side().wait_send()
    for slot in range(1, slots):
        for half in (0, 1):
            token_copy(slot, half).wait_send()
    for i in range(count):
        for hop in range(1, nz):
            sent(i, hop)
        if i > 1:
            term_copy(i, 1).wait_send()
            if items[i][1]:
                term_copy(i, 0).wait_send()


def on_device(tokens, partner_bits, w_up, w_down):
    dp, rank = lax.axis_size("dp"), lax.axis_index("tensor")
    nz = dp // 2
    slots = w_up.shape[1]
    rows, width = tokens.shape
    rows_up, hidden = w_up.shape[2], w_up.shape[3]
    rows_down = w_down.shape[2]
    half = hidden // 2
    my_bits = lax.dynamic_slice_in_dim(partner_bits, rank, 1, 0)[0]
    order = jnp.sum(
        (my_bits[None, :] == jnp.arange(slots - 1, dtype=jnp.int32)[:, None])
        * jnp.arange(1, slots, dtype=jnp.int32)[None, :], axis=1,
    )

    def by_bit(weights):
        picked = [weights[0]]
        for bit in range(slots - 1):
            choice = weights[1]
            for slot in range(2, slots):
                choice = jnp.where(order[bit] == slot, weights[slot], choice)
            picked.append(choice)
        return jnp.stack(picked)

    up = by_bit(w_up[0]).reshape(slots, rows_up, nz, 2, hidden // dp)
    up = up.transpose(3, 0, 1, 2, 4).reshape(2, slots, rows_up, half)
    down = by_bit(w_down[0])
    items = item_list(slots, width)
    count = len(items)
    kind = tokens.dtype
    dma = pltpu.SemaphoreType.DMA
    return pl.pallas_call(
        functools.partial(kernel, nz, items),
        out_shape=jax.ShapeDtypeStruct((rows, width), kind),
        in_specs=[pl.BlockSpec(memory_space=pltpu.VMEM)] * 3,
        out_specs=pl.BlockSpec(memory_space=pltpu.VMEM),
        scratch_shapes=[
            pltpu.VMEM((slots, 2, rows, width), kind),
            pltpu.VMEM((slots, width, half), kind),
            pltpu.VMEM((slots, half, width), kind),
            pltpu.VMEM((2, rows, half), kind),
            pltpu.VMEM((slots, 2, rows, width), kind),
            pltpu.VMEM((slots, 2, rows, width), kind),
            pltpu.VMEM((rows, width), jnp.float32),
            dma((count, 2, nz - 1)),
            dma((count, 2, nz - 1)),
            dma((3,)),
            dma,
            dma,
            dma((slots, 2)),
            dma((slots, 2)),
            dma((count, 2)),
            dma((count, 2)),
        ],
        compiler_params=pltpu.CompilerParams(
            collective_id=0, has_side_effects=True, vmem_limit_bytes=48 << 20
        ),
    )(tokens, up, down)


def solution(mesh):
    in_specs = (
        P("dp", "tensor"),
        P(),
        P("tensor", None, "dp", None),
        P("tensor", None, "dp", None),
    )
    return jax.shard_map(
        on_device, mesh=mesh, in_specs=in_specs, out_specs=P("dp", "tensor"), check_vma=False
    )
```

time: 159 us -> 82.3 us (0.52)
  waiting for transfers between devices: 131 us -> 0 us
  Pallas kernels: 0 us -> 74.6 us
  between operations: 13.5 us -> 1.38 us
  matrix products: 7.96 us -> 0 us
  starting transfers between devices: 4.71 us -> 0 us
  local copies, waits for them, and re-layouts: 0.27 us -> 4.48 us
    all_gather x2 -> x0, waiting for transfers between devices: 111 us -> none  [the longest x1 60.9 us: on_device(): lax.all_gather(w_down, 'dp', axis=2, tiled=True)[0]]
    pallas_call x0 -> x1, Pallas kernels: none -> 74.6 us  [on_device(): pl.pallas_call(functools.partial(kernel, nz, items), out_shape=jax.ShapeD...]
    ppermute x4 -> x0, waiting for transfers between devices: 18.5 us -> none  [swapped(): return lax.ppermute(block, axis, route)]
    dot_general x3 -> x0, matrix products: 7.96 us -> none  [the longest x1 5.59 us: on_device(): jnp.einsum('tf,sfd->std', columns, lax.all_gather(w_down, 'dp', axis=2, t...]
    ppermute x4 -> x0, starting transfers between devices: 4.67 us -> none  [swapped(): return lax.ppermute(block, axis, route)]
    unnamed x2 -> x7, local copies, waits for them, and re-layouts: 0.01 us -> 3.2 us
  transfers between devices with their start and end apart: 6 -> 0, of which waited for: 5 -> 0; matrix products, arithmetic and copies ran while one was open for 1% -> 0% of each run, Pallas kernels for 0% -> 0%
where the time goes in v1:
time: 82.3 us; the launch traced here: 82.1 us
  Pallas kernels  74.6 us (91%)
  local copies, waits for them, and re-layouts  4.48 us (5%)
  other arithmetic  1.57 us (2%)
  between operations  1.38 us (2%)
    pallas_call x1, Pallas kernels, on_device(): pl.pallas_call(functools.partial(kernel, nz, items), out_shape=jax.ShapeD...  74.6 us
    unnamed x7, local copies, waits for them, and re-layouts  3.2 us

profile of v1, /device:TPU:0, one launch (start us, length us, event | category | flops | bytes accessed | tf_op | source)
XLA Modules:
  0.0 82.1 jit_solution(14993290310776784032)
XLA Ops:
  0.0 0.0 copy-start
  0.0 0.7 copy-done
  0.7 0.2 dynamic-slice_reduce_fusion
  0.9 0.1 fusion
  1.0 0.6 fusion.2
  2.9 1.1 %slice_bitcast_fusion = (bf16[1,128,512]{2,1,0:T(8,128)(2,1)S(1)}, bf16[1,128,512]{2,1,0:T(8,128)(2,1)S(1)}, bf16[1,128,512]{2,1,0:T(8,128)(2,1)S(1)}) fusion(bf16[1,3,128,512]{3,2,1,0:T(8,128)(2,1)} %param.7, pred[]{:T(512)} %bitcast, pred[]{:T(512)} %bitcast.1), kind=kLoop, calls=%fused_computation.4 | loop fusion | flops 131072 | bytes 786434 | tf_op jit(solution)/shard_map/slice | solution.py:256
  4.0 0.0 copy-start.2
  4.0 0.9 %copy-done.2 = bf16[1,3,64,1024]{3,2,1,0:T(8,128)(2,1)S(1)} copy-done((bf16[1,3,64,1024]{3,2,1,0:T(8,128)(2,1)S(1)}, bf16[1,3,64,1024]{3,2,1,0:T(8,128)(2,1)}, u32[]{:S(2)}) %copy-start.2) | copy-done | bytes 393240
  5.0 0.1 stack.12
  5.1 0.1 select_n.76
  5.2 0.1 select_n.79
  5.4 0.3 maximum_bitcast_fusion
  5.7 0.0 copy-start.1
  5.7 0.2 reshape.106.up_ref
  5.8 0.8 %copy-done.1 = bf16[384,512]{1,0:T(8,128)(2,1)S(1)} copy-done((bf16[384,512]{1,0:T(8,128)(2,1)S(1)}, bf16[384,512]{1,0:T(8,128)(2,1)}, u32[]{:S(2)}) %copy-start.1) | copy-done | bytes 393240
  6.7 74.6 %shard_map.46 = bf16[384,512]{1,0:T(8,128)(2,1)S(1)} custom-call(bf16[384,512]{1,0:T(8,128)(2,1)S(1)} %copy-done.1, bf16[2,3,64,512]{3,2,1,0:T(8,128)(2,1)S(1)} %reshape.106.up_ref, bf16[3,128,512]{2,1,0:T(8,128)(2,1)S(1)} %pad_maximum_fusion.down_ref), custom_call_target="tpu_custom_call" | custom-call | tf_op jit(solution)/shard_map/pallas_call | solution.py:271
  81.3 0.7 copy.12
  (6 shorter events, 0.2 us)
Async XLA Ops:
  0.0 0.7 copy-start
  4.0 1.0 %copy-start.2 = (bf16[1,3,64,1024]{3,2,1,0:T(8,128)(2,1)S(1)}, bf16[1,3,64,1024]{3,2,1,0:T(8,128)(2,1)}, u32[]{:S(2)}) copy-start(bf16[1,3,64,1024]{3,2,1,0:T(8,128)(2,1)} %param.6) | copy-start | bytes 1179652
  5.7 1.0 %copy-start.1 = (bf16[384,512]{1,0:T(8,128)(2,1)S(1)}, bf16[384,512]{1,0:T(8,128)(2,1)}, u32[]{:S(2)}) copy-start(bf16[384,512]{1,0:T(8,128)(2,1)} %tok_ref.1) | copy-start | bytes 1179652

commit v2 on v1

--- a/solution.py
+++ b/solution.py
@@ -22,13 +22,13 @@
 
 
 def kernel(
-    nz, items, tok_ref, up_ref, down_ref, out_ref,
-    tok, up, down, hid, stage, landed, own,
+    nz, items, bits_ref, tok_ref, up_raw, down_raw, out_ref,
+    tok, up, down, hid, stage, landed, own, up_in, down_in, up_away,
     line_send, line_recv, local_sem, side_send, side_recv,
     tok_send, tok_recv, term_send, term_recv,
 ):
     slots = tok.shape[0]
-    rows_up, rows_down = up_ref.shape[2], down_ref.shape[1]
+    rows_up, rows_down, strip = up_raw.shape[2], down_raw.shape[2], up_raw.shape[3] // (2 * nz)
     me, rank = lax.axis_index("dp"), lax.axis_index("tensor")
     z, x = me // 2, me % 2
     other = z * 2 + (1 - x)
@@ -36,12 +36,36 @@
     for bit in range(slots - 1):
         partner.append(rank + (1 - 2 * ((rank // (1 << bit)) % 2)) * (1 << bit))
 
+    fetch_up = pltpu.make_async_copy(up_raw.at[0], up_in, local_sem.at[0])
+    fetch_down = pltpu.make_async_copy(down_raw.at[0], down_in, local_sem.at[1])
+    mine = pltpu.make_async_copy(tok_ref, tok.at[0, x], local_sem.at[2])
+    fetch_up.start()
+    fetch_down.start()
+    mine.start()
     barrier = pltpu.get_barrier_semaphore()
     greeted = [((((z + 1) % nz) * 2 + x), rank), (((z + nz - 1) % nz) * 2 + x, rank), (other, rank)]
     for slot in range(1, slots):
         greeted += [(me, partner[slot]), (other, partner[slot])]
     for device in greeted:
         pl.semaphore_signal(barrier, inc=1, device_id=device, device_id_type=MESH)
+    bits = [jnp.clip(bits_ref[rank, slot], 0, slots - 2) for slot in range(slots - 1)]
+    fetch_up.wait()
+    own_row = pl.multiple_of((z * 2 + x) * rows_up, rows_up)
+    for strip_z in range(nz):
+        columns = slice(strip_z * strip, (strip_z + 1) * strip)
+        even, odd = (
+            up_in[:, :, (2 * strip_z + at) * strip:(2 * strip_z + at + 1) * strip] for at in (0, 1)
+        )
+        up_away[:, :, columns] = jnp.where(x == 0, odd, even)
+        up[:, pl.ds(own_row, rows_up), columns] = jnp.where(x == 0, even, odd)
+    fetch_down.wait()
+    down_row = pl.multiple_of(z * rows_down, rows_down)
+    for bit in range(slots - 1):
+        pick = jnp.int32(0)
+        for slot in range(slots - 1):
+            pick += jnp.where(bits[slot] == bit, slot + 1, 0)
+        down[bit + 1, pl.ds(down_row, rows_down), :] = down_in[jnp.minimum(pick, slots - 1)]
+    down[0, pl.ds(down_row, rows_down), :] = down_in[0]
     pl.semaphore_wait(barrier, len(greeted))
 
     def up_rows(at_z, at_x):
@@ -54,19 +78,11 @@
         row = pl.multiple_of(at_z * rows_down, rows_down)
         return down.at[which, pl.ds(row, rows_down), pl.ds(first, width)]
 
-    def source(item, hop, at_z):
-        kind, which, first, width = item
-        if hop > 1 or (kind == "up" and which == 1):
-            return place(item, at_z)
-        if kind == "up":
-            return up_ref.at[x]
-        return down_ref.at[which, :, pl.ds(first, width)]
-
     def line(i, hop, way):
         sign = 1 - 2 * way
         origin = z - sign * (hop - 1)
         return pltpu.make_async_remote_copy(
-            src_ref=source(items[i], hop, origin),
+            src_ref=place(items[i], origin),
             dst_ref=place(items[i], origin),
             send_sem=line_send.at[i, way, hop - 1],
             recv_sem=line_recv.at[i, way, hop - 1],
@@ -110,7 +126,7 @@
 
     def side(dst_x):
         return pltpu.make_async_remote_copy(
-            src_ref=up_ref.at[1 - x], dst_ref=up_rows(z, dst_x),
+            src_ref=up_away, dst_ref=up_rows(z, dst_x),
             send_sem=side_send, recv_sem=side_recv,
             device_id=(other, rank), device_id_type=MESH,
         )
@@ -147,19 +163,8 @@
     token_side().start()
     for slot in range(slots - 1, 0, -1):
         token_copy(slot, 0).start()
-    mine = [
-        pltpu.make_async_copy(tok_ref, tok.at[0, x], local_sem.at[0]),
-        pltpu.make_async_copy(up_ref.at[x], up_rows(z, x), local_sem.at[1]),
-        pltpu.make_async_copy(
-            down_ref, down.at[:, pl.ds(pl.multiple_of(z * rows_down, rows_down), rows_down), :], local_sem.at[2]
-        ),
-    ]
-    for copy in mine:
-        copy.start()
-
     def make_hidden():
-        for copy in mine:
-            copy.wait()
+        mine.wait()
         for slot in range(1, slots):
             for half in (0, 1):
                 token_copy(slot, half).wait_recv()
@@ -167,7 +172,7 @@
         def one(half, carry):
             pre = jnp.dot(tok[0, half], up[0], preferred_element_type=jnp.float32)
             for slot in range(1, slots):
-                pre += jnp.dot(tok[slot, half], up[slot], preferred_element_type=jnp.float32)
+                pre += jnp.dot(tok[1 + bits[slot - 1], half], up[slot], preferred_element_type=jnp.float32)
             hid[half] = jax.nn.gelu(pre, approximate=True).astype(hid.dtype)
             return carry
 
@@ -239,31 +244,12 @@
 
 
 def on_device(tokens, partner_bits, w_up, w_down):
-    dp, rank = lax.axis_size("dp"), lax.axis_index("tensor")
-    nz = dp // 2
+    nz = lax.axis_size("dp") // 2
     slots = w_up.shape[1]
     rows, width = tokens.shape
     rows_up, hidden = w_up.shape[2], w_up.shape[3]
     rows_down = w_down.shape[2]
     half = hidden // 2
-    my_bits = lax.dynamic_slice_in_dim(partner_bits, rank, 1, 0)[0]
-    order = jnp.sum(
-        (my_bits[None, :] == jnp.arange(slots - 1, dtype=jnp.int32)[:, None])
-        * jnp.arange(1, slots, dtype=jnp.int32)[None, :], axis=1,
-    )
-
-    def by_bit(weights):
-        picked = [weights[0]]
-        for bit in range(slots - 1):
-            choice = weights[1]
-            for slot in range(2, slots):
-                choice = jnp.where(order[bit] == slot, weights[slot], choice)
-            picked.append(choice)
-        return jnp.stack(picked)
-
-    up = by_bit(w_up[0]).reshape(slots, rows_up, nz, 2, hidden // dp)
-    up = up.transpose(3, 0, 1, 2, 4).reshape(2, slots, rows_up, half)
-    down = by_bit(w_down[0])
     items = item_list(slots, width)
     count = len(items)
     kind = tokens.dtype
@@ -271,7 +257,7 @@
     return pl.pallas_call(
         functools.partial(kernel, nz, items),
         out_shape=jax.ShapeDtypeStruct((rows, width), kind),
-        in_specs=[pl.BlockSpec(memory_space=pltpu.VMEM)] * 3,
+        in_specs=[pl.BlockSpec(memory_space=pltpu.SMEM)] + [pl.BlockSpec(memory_space=pl.ANY)] * 3,
         out_specs=pl.BlockSpec(memory_space=pltpu.VMEM),
         scratch_shapes=[
             pltpu.VMEM((slots, 2, rows, width), kind),
@@ -281,6 +267,9 @@
             pltpu.VMEM((slots, 2, rows, width), kind),
             pltpu.VMEM((slots, 2, rows, width), kind),
             pltpu.VMEM((rows, width), jnp.float32),
+            pltpu.VMEM(w_up.shape[1:], kind),
+            pltpu.VMEM(w_down.shape[1:], kind),
+            pltpu.VMEM((slots, rows_up, half), kind),
             dma((count, 2, nz - 1)),
             dma((count, 2, nz - 1)),
             dma((3,)),
@@ -292,9 +281,9 @@
             dma((count, 2)),
         ],
         compiler_params=pltpu.CompilerParams(
-            collective_id=0, has_side_effects=True, vmem_limit_bytes=48 << 20
+            collective_id=0, has_side_effects=True, vmem_limit_bytes=67043328
         ),
-    )(tokens, up, down)
+    )(partner_bits, tokens, w_up, w_down)
 
 
 def solution(mesh):

time: 82.3 us -> 79.5 us (0.966)
  other arithmetic: 1.57 us -> 0 us
  Pallas kernels: 74.6 us -> 76.1 us
  local copies, waits for them, and re-layouts: 4.48 us -> 3.1 us
  between operations: 1.38 us -> 0.01 us
    pallas_call x1, Pallas kernels: 74.6 us -> 76.1 us  [on_device(): pl.pallas_call(functools.partial(kernel, nz, items), out_shape=jax.ShapeD...]
    slice x2 -> x0, other arithmetic: 1.09 us -> none  [by_bit(): picked = [weights[0]]]
    unnamed x7 -> x2, local copies, waits for them, and re-layouts: 3.2 us -> 3.1 us
where the time goes in v2:
time: 79.5 us; the launch traced here: 79.2 us
  Pallas kernels  76.1 us (96%)
  local copies, waits for them, and re-layouts  3.1 us (4%)
    pallas_call x1, Pallas kernels, on_device(): pl.pallas_call(functools.partial(kernel, nz, items), out_shape=jax.ShapeD...  76.1 us
    unnamed x2, local copies, waits for them, and re-layouts  3.1 us

profile of v2, /device:TPU:0, one launch (start us, length us, event | category | flops | bytes accessed | tf_op | source)
XLA Modules:
  0.0 79.2 jit_solution(7789583132233894061)
XLA Ops:
  0.0 1.3 %copy.5.bits_ref = s32[4,2]{1,0:T(4,128)} copy(s32[4,2]{0,1:T(2,128)} %param.5) | data formatting | bytes 64 | tf_op args[1]
  1.3 76.1 %shard_map.46 = bf16[384,512]{1,0:T(8,128)(2,1)} custom-call(s32[4,2]{1,0:T(4,128)} %copy.5.bits_ref, bf16[384,512]{1,0:T(8,128)(2,1)} %tok_ref.1, bf16[1,3,64,1024]{3,2,1,0:T(8,128)(2,1)} %up_raw.1, bf16[1,3,128,512]{3,2,1,0:T(8,128)(2,1)} %down_raw.1), custom_call_target="tpu_custom_call" | custom-call | tf_op jit(solution)/shard_map/pallas_call | solution.py:257
  77.5 1.8 %copy.7 = bf16[384,512]{1,0:T(8,128)(2,1)} copy(bf16[384,512]{1,0:T(8,128)(2,1)} %shard_map.46) | data formatting | bytes 786432

commit v3 on v2

--- a/solution.py
+++ b/solution.py
@@ -8,24 +8,19 @@
 from jax.sharding import PartitionSpec as P
 
 MESH = pl.DeviceIdType.MESH
-OWN_CHUNKS = 2
-
-
-def item_list(slots, width):
-    items = [("up", 0, 0, 0), ("up", 1, 0, 0)]
-    for slot in range(slots - 1, 0, -1):
-        items.append(("down", slot, 0, width))
-    part = width // OWN_CHUNKS
-    for chunk in range(OWN_CHUNKS):
-        items.append(("down", 0, chunk * part, part))
-    return items
+CHUNKS = 2
+
+
+def item_list(width):
+    part = width // CHUNKS
+    return [("up", 0, 0), ("up", 1, 0)] + [("down", c * part, part) for c in range(CHUNKS)]
 
 
 def kernel(
     nz, items, bits_ref, tok_ref, up_raw, down_raw, out_ref,
-    tok, up, down, hid, stage, landed, own, up_in, down_in, up_away,
+    tok, up, down, hid, stage, landed, own, up_in, down_in, up_away, down_away,
     line_send, line_recv, local_sem, side_send, side_recv,
-    tok_send, tok_recv, term_send, term_recv,
+    tok_send, tok_recv, down_send, down_recv, hid_send, hid_recv, sum_send, sum_recv,
 ):
     slots = tok.shape[0]
     rows_up, rows_down, strip = up_raw.shape[2], down_raw.shape[2], up_raw.shape[3] // (2 * nz)
@@ -48,7 +43,7 @@
         greeted += [(me, partner[slot]), (other, partner[slot])]
     for device in greeted:
         pl.semaphore_signal(barrier, inc=1, device_id=device, device_id_type=MESH)
-    bits = [jnp.clip(bits_ref[rank, slot], 0, slots - 2) for slot in range(slots - 1)]
+    bits = [jnp.clip(bits_ref[slot, rank], 0, slots - 2) for slot in range(slots - 1)]
     fetch_up.wait()
     own_row = pl.multiple_of((z * 2 + x) * rows_up, rows_up)
     for strip_z in range(nz):
@@ -64,7 +59,7 @@
         pick = jnp.int32(0)
         for slot in range(slots - 1):
             pick += jnp.where(bits[slot] == bit, slot + 1, 0)
-        down[bit + 1, pl.ds(down_row, rows_down), :] = down_in[jnp.minimum(pick, slots - 1)]
+        down_away[bit] = down_in[jnp.minimum(pick, slots - 1)]
     down[0, pl.ds(down_row, rows_down), :] = down_in[0]
     pl.semaphore_wait(barrier, len(greeted))
 
@@ -72,11 +67,11 @@
         return up.at[:, pl.ds(pl.multiple_of((at_z * 2 + at_x) * rows_up, rows_up), rows_up), :]
 
     def place(item, at_z):
-        kind, which, first, width = item
+        kind, first, width = item
         if kind == "up":
-            return up_rows(at_z, x if which == 0 else 1 - x)
+            return up_rows(at_z, x if first == 0 else 1 - x)
         row = pl.multiple_of(at_z * rows_down, rows_down)
-        return down.at[which, pl.ds(row, rows_down), pl.ds(first, width)]
+        return down.at[:, pl.ds(row, rows_down), pl.ds(first, width)]
 
     def line(i, hop, way):
         sign = 1 - 2 * way
@@ -147,100 +142,121 @@
             device_id=(other, rank), device_id_type=MESH,
         )
 
-    def term_copy(i, far):
-        unused, slot, first, width = items[i]
-        columns = pl.ds(first, width)
-        return pltpu.make_async_remote_copy(
-            src_ref=stage.at[slot, 1 - x if far else x, :, columns],
-            dst_ref=landed.at[slot, x, :, columns],
-            send_sem=term_send.at[i, far], recv_sem=term_recv.at[i, far],
-            device_id=(other if far else me, partner[slot]), device_id_type=MESH,
-        )
-
-    last = nz - 1
+    def down_copy(slot):
+        return pltpu.make_async_remote_copy(
+            src_ref=down_away.at[slot - 1], dst_ref=down.at[slot, pl.ds(down_row, rows_down), :],
+            send_sem=down_send.at[slot], recv_sem=down_recv.at[slot],
+            device_id=(me, partner[slot]), device_id_type=MESH,
+        )
+
+    def hid_copy(slot, far):
+        at = 1 - x if far else x
+        return pltpu.make_async_remote_copy(
+            src_ref=hid.at[0, at], dst_ref=hid.at[slot, at],
+            send_sem=hid_send.at[slot, far], recv_sem=hid_recv.at[slot, far],
+            device_id=(me, partner[slot]), device_id_type=MESH,
+        )
+
+    def sum_copy(i):
+        columns = pl.ds(items[i][1], items[i][2])
+        return pltpu.make_async_remote_copy(
+            src_ref=stage.at[:, columns], dst_ref=landed.at[:, columns],
+            send_sem=sum_send.at[i], recv_sem=sum_recv.at[i],
+            device_id=(other, rank), device_id_type=MESH,
+        )
+
     send(0, 1)
     side(x).start()
     token_side().start()
     for slot in range(slots - 1, 0, -1):
         token_copy(slot, 0).start()
+    for slot in range(slots - 1, 0, -1):
+        down_copy(slot).start()
     def make_hidden():
         mine.wait()
         for slot in range(1, slots):
             for half in (0, 1):
                 token_copy(slot, half).wait_recv()
 
-        def one(half, carry):
+        def one(step, carry):
+            half = (1 - x) * (1 - step) + x * step
             pre = jnp.dot(tok[0, half], up[0], preferred_element_type=jnp.float32)
             for slot in range(1, slots):
                 pre += jnp.dot(tok[1 + bits[slot - 1], half], up[slot], preferred_element_type=jnp.float32)
-            hid[half] = jax.nn.gelu(pre, approximate=True).astype(hid.dtype)
+            hid[0, half] = jax.nn.gelu(pre, approximate=True).astype(hid.dtype)
             return carry
 
         lax.fori_loop(0, 2, one, 0)
-
-    def make_terms(i):
-        unused, slot, first, width = items[i]
+        for far in (1, 0):
+            for slot in range(slots - 1, 0, -1):
+                hid_copy(slot, far).start()
+
+    def product(at, columns):
+        total = jnp.dot(hid[0, at], down[0, :, columns], preferred_element_type=jnp.float32)
+        for slot in range(1, slots):
+            total += jnp.dot(hid[slot, at], down[slot, :, columns], preferred_element_type=jnp.float32)
+        return total
+
+    def make_away(i):
+        unused, first, width = items[i]
         columns = slice(first, first + width)
-
-        def term(half):
-            return jnp.dot(hid[half], down[slot, :, columns], preferred_element_type=jnp.float32)
-
-        stage[slot, 1 - x, :, columns] = term(1 - x).astype(stage.dtype)
-        term_copy(i, 1).start()
-        if slot == 0:
-            own[:, columns] = term(x)
-        else:
-            stage[slot, x, :, columns] = term(x).astype(stage.dtype)
-            term_copy(i, 0).start()
+        if first == 0:
+            for slot in range(1, slots):
+                hid_copy(slot, 1).wait_recv()
+        stage[:, columns] = product(1 - x, columns).astype(stage.dtype)
+        sum_copy(i).start()
+
+    def complete(i):
+        arrive(i, nz - 1)
+        if i == 1:
+            make_hidden()
+        if i > 1:
+            make_away(i)
+
+    def first_send(i):
+        if i >= count:
+            return
+        if i == 1:
+            side(1 - x).wait_recv()
+        if i == 2:
+            for slot in range(1, slots):
+                down_copy(slot).wait_recv()
+        send(i, 1)
 
     count = len(items)
-    for step in range(count + last):
-        for hop in range(1, nz + 1):
-            i = step - (hop - 1)
-            if not 0 <= i < count:
-                continue
-            if hop > 1:
-                arrive(i, hop - 1)
-            elif i == 1:
-                side(1 - x).wait_recv()
-            if hop < nz:
-                if (i, hop) != (0, 1):
-                    send(i, hop)
-        if step == 1:
+    for i in range(count):
+        first_send(i + 1)
+        for hop in range(1, nz):
+            if hop < nz - 1:
+                arrive(i, hop)
+                send(i, hop + 1)
+            if hop == 1 and i > 0:
+                complete(i - 1)
+        if i == 0:
             token_side().wait_recv()
             for slot in range(slots - 1, 0, -1):
                 token_copy(slot, 1).start()
-        i = step - last
-        if i == 1:
-            make_hidden()
-        if i > 1:
-            make_terms(i)
-
+    complete(count - 1)
+    for slot in range(1, slots):
+        hid_copy(slot, 0).wait_recv()
+    own[...] = product(x, slice(None))
     for i in range(2, count):
-        unused, slot, first, width = items[i]
-        term_copy(i, 1).wait_recv()
-        if slot:
-            term_copy(i, 0).wait_recv()
-            continue
-        columns = slice(first, first + width)
-        total = own[:, columns] + landed[0, 1 - x, :, columns].astype(jnp.float32)
-        for slot in range(1, slots):
-            for half in (0, 1):
-                total += landed[slot, half, :, columns].astype(jnp.float32)
-        out_ref[:, columns] = total.astype(out_ref.dtype)
+        sum_copy(i).wait_recv()
+        columns = slice(items[i][1], items[i][1] + items[i][2])
+        out_ref[:, columns] = (own[:, columns] + landed[:, columns].astype(jnp.float32)).astype(out_ref.dtype)
 
     side(x).wait_send()
     token_side().wait_send()
     for slot in range(1, slots):
+        down_copy(slot).wait_send()
         for half in (0, 1):
             token_copy(slot, half).wait_send()
+            hid_copy(slot, half).wait_send()
     for i in range(count):
         for hop in range(1, nz):
             sent(i, hop)
         if i > 1:
-            term_copy(i, 1).wait_send()
-            if items[i][1]:
-                term_copy(i, 0).wait_send()
+            sum_copy(i).wait_send()
 
 
 def on_device(tokens, partner_bits, w_up, w_down):
@@ -250,7 +266,7 @@
     rows_up, hidden = w_up.shape[2], w_up.shape[3]
     rows_down = w_down.shape[2]
     half = hidden // 2
-    items = item_list(slots, width)
+    items = item_list(width)
     count = len(items)
     kind = tokens.dtype
     dma = pltpu.SemaphoreType.DMA
@@ -263,13 +279,14 @@
             pltpu.VMEM((slots, 2, rows, width), kind),
             pltpu.VMEM((slots, width, half), kind),
             pltpu.VMEM((slots, half, width), kind),
-            pltpu.VMEM((2, rows, half), kind),
-            pltpu.VMEM((slots, 2, rows, width), kind),
-            pltpu.VMEM((slots, 2, rows, width), kind),
+            pltpu.VMEM((slots, 2, rows, half), kind),
+            pltpu.VMEM((rows, width), kind),
+            pltpu.VMEM((rows, width), kind),
             pltpu.VMEM((rows, width), jnp.float32),
             pltpu.VMEM(w_up.shape[1:], kind),
             pltpu.VMEM(w_down.shape[1:], kind),
             pltpu.VMEM((slots, rows_up, half), kind),
+            pltpu.VMEM((slots - 1,) + w_down.shape[2:], kind),
             dma((count, 2, nz - 1)),
             dma((count, 2, nz - 1)),
             dma((3,)),
@@ -277,13 +294,17 @@
             dma,
             dma((slots, 2)),
             dma((slots, 2)),
-            dma((count, 2)),
-            dma((count, 2)),
+            dma((slots,)),
+            dma((slots,)),
+            dma((slots, 2)),
+            dma((slots, 2)),
+            dma((count,)),
+            dma((count,)),
         ],
         compiler_params=pltpu.CompilerParams(
             collective_id=0, has_side_effects=True, vmem_limit_bytes=67043328
         ),
-    )(partner_bits, tokens, w_up, w_down)
+    )(partner_bits.T, tokens, w_up, w_down)
 
 
 def solution(mesh):

time: 79.5 us -> 67.1 us (0.84)
  Pallas kernels: 76.1 us -> 65.1 us
  local copies, waits for them, and re-layouts: 3.1 us -> 1.77 us
    pallas_call x1, Pallas kernels: 76.1 us -> 65.1 us  [on_device(): pl.pallas_call(functools.partial(kernel, nz, items), out_shape=jax.ShapeD...]
    unnamed x2 -> x1, local copies, waits for them, and re-layouts: 3.1 us -> 1.77 us
where the time goes in v3:
time: 67.1 us; the launch traced here: 66.9 us
  Pallas kernels  65.1 us (97%)
  local copies, waits for them, and re-layouts  1.77 us (3%)
    pallas_call x1, Pallas kernels, on_device(): pl.pallas_call(functools.partial(kernel, nz, items), out_shape=jax.ShapeD...  65.1 us
    unnamed x1, local copies, waits for them, and re-layouts  1.77 us

profile of v3, /device:TPU:0, one launch (start us, length us, event | category | flops | bytes accessed | tf_op | source)
XLA Modules:
  0.0 66.9 jit_solution(3703885795631418903)
XLA Ops:
  0.0 65.1 %shard_map.46 = bf16[384,512]{1,0:T(8,128)(2,1)} custom-call(s32[2,4]{1,0:T(2,128)} %bitcast.1, bf16[384,512]{1,0:T(8,128)(2,1)} %tok_ref.1, bf16[1,3,64,1024]{3,2,1,0:T(8,128)(2,1)} %up_raw.1, bf16[1,3,128,512]{3,2,1,0:T(8,128)(2,1)} %down_raw.1), custom_call_target="tpu_custom_call" | custom-call | tf_op jit(solution)/shard_map/pallas_call | solution.py:273
  65.1 1.8 %copy.6 = bf16[384,512]{1,0:T(8,128)(2,1)} copy(bf16[384,512]{1,0:T(8,128)(2,1)} %shard_map.46) | data formatting | bytes 786432

commit v4 on v3

--- a/solution.py
+++ b/solution.py
@@ -8,12 +8,15 @@
 from jax.sharding import PartitionSpec as P
 
 MESH = pl.DeviceIdType.MESH
-CHUNKS = 2
+CHUNKS = (2, 4, 4)
 
 
 def item_list(width):
-    part = width // CHUNKS
-    return [("up", 0, 0), ("up", 1, 0)] + [("down", c * part, part) for c in range(CHUNKS)]
+    items, first = [("up", 0, 0), ("up", 1, 0)], 0
+    for share in CHUNKS:
+        items.append(("down", first, width // share))
+        first += width // share
+    return items
 
 
 def kernel(
@@ -43,6 +46,7 @@
         greeted += [(me, partner[slot]), (other, partner[slot])]
     for device in greeted:
         pl.semaphore_signal(barrier, inc=1, device_id=device, device_id_type=MESH)
+    down_row = pl.multiple_of(z * rows_down, rows_down)
     bits = [jnp.clip(bits_ref[slot, rank], 0, slots - 2) for slot in range(slots - 1)]
     fetch_up.wait()
     own_row = pl.multiple_of((z * 2 + x) * rows_up, rows_up)
@@ -53,14 +57,6 @@
         )
         up_away[:, :, columns] = jnp.where(x == 0, odd, even)
         up[:, pl.ds(own_row, rows_up), columns] = jnp.where(x == 0, even, odd)
-    fetch_down.wait()
-    down_row = pl.multiple_of(z * rows_down, rows_down)
-    for bit in range(slots - 1):
-        pick = jnp.int32(0)
-        for slot in range(slots - 1):
-            pick += jnp.where(bits[slot] == bit, slot + 1, 0)
-        down_away[bit] = down_in[jnp.minimum(pick, slots - 1)]
-    down[0, pl.ds(down_row, rows_down), :] = down_in[0]
     pl.semaphore_wait(barrier, len(greeted))
 
     def up_rows(at_z, at_x):
@@ -170,6 +166,13 @@
     token_side().start()
     for slot in range(slots - 1, 0, -1):
         token_copy(slot, 0).start()
+    fetch_down.wait()
+    for bit in range(slots - 1):
+        pick = jnp.int32(0)
+        for slot in range(slots - 1):
+            pick += jnp.where(bits[slot] == bit, slot + 1, 0)
+        down_away[bit] = down_in[jnp.minimum(pick, slots - 1)]
+    down[0, pl.ds(down_row, rows_down), :] = down_in[0]
     for slot in range(slots - 1, 0, -1):
         down_copy(slot).start()
     def make_hidden():

time: 67.1 us -> 66.1 us (0.985)
  Pallas kernels: 65.1 us -> 64.2 us
    pallas_call x1, Pallas kernels: 65.1 us -> 64.2 us  [on_device(): pl.pallas_call(functools.partial(kernel, nz, items), out_shape=jax.ShapeD...]
where the time goes in v4:
time: 66.1 us; the launch traced here: 66 us
  Pallas kernels  64.2 us (97%)
  local copies, waits for them, and re-layouts  1.77 us (3%)
    pallas_call x1, Pallas kernels, on_device(): pl.pallas_call(functools.partial(kernel, nz, items), out_shape=jax.ShapeD...  64.2 us
    unnamed x1, local copies, waits for them, and re-layouts  1.77 us

profile of v4, /device:TPU:0, one launch (start us, length us, event | category | flops | bytes accessed | tf_op | source)
XLA Modules:
  0.0 66.0 jit_solution(9634765558205695127)
XLA Ops:
  0.0 64.2 %shard_map.46 = bf16[384,512]{1,0:T(8,128)(2,1)} custom-call(s32[2,4]{1,0:T(2,128)} %bitcast.1, bf16[384,512]{1,0:T(8,128)(2,1)} %tok_ref.1, bf16[1,3,64,1024]{3,2,1,0:T(8,128)(2,1)} %up_raw.1, bf16[1,3,128,512]{3,2,1,0:T(8,128)(2,1)} %down_raw.1), custom_call_target="tpu_custom_call" | custom-call | tf_op jit(solution)/shard_map/pallas_call | solution.py:276
  64.2 1.8 %copy.6 = bf16[384,512]{1,0:T(8,128)(2,1)} copy(bf16[384,512]{1,0:T(8,128)(2,1)} %shard_map.46) | data formatting | bytes 786432
